TPU v7x, 128 devices: a whole 4x4x4 slice. The times are simulated.
128 devices in a mesh: blk: 32 (over z_hi, y, x), head: 4 (over z_lo, core).
Axes of the slice: x: 4, y: 4, z: 4 (z_hi: 2, z_lo: 2; z = z_hi * 2 + z_lo), core: 2. Of those that a mesh axis runs over, the one named last changes fastest.
Arguments:
- tokens: bfloat16 [12288, 1024], P(('blk', 'head')), may hold values from -18 to 18
- block_order: int32 [64], replicated, may hold values from 0 to 63, as said below
- request_lengths: int32 [9], replicated, may hold values from 1 to 9216, 12288 in all
- enc_lengths: int32 [9], replicated, may hold values from 1 to 512, 2048 in all
- w_qkv: bfloat16 [3, 1024, 1024], P(None, None, 'head'), may hold values from -0.1875 to 0.1875
- w_out: bfloat16 [1024, 1024], P('head'), may hold values from -0.1875 to 0.1875
- enc_kv: bfloat16 [2, 2048, 1024], P(None, 'blk', 'head'), may hold values from -18 to 18
- w_cq: bfloat16 [1024, 1024], replicated, may hold values from -0.1875 to 0.1875
- w_co: bfloat16 [1024, 1024], replicated, may hold values from -0.1875 to 0.1875
- w_up: bfloat16 [1024, 4096], replicated, may hold values from -0.1875 to 0.1875
- w_down: bfloat16 [4096, 1024], replicated, may hold values from -0.09375 to 0.09375
- w_next: bfloat16 [3, 1024, 1024], P(None, None, 'head'), may hold values from -0.1875 to 0.1875
Outputs:
- output: float32 [12288, 1024], P(('blk', 'head'))
- cache: bfloat16 [2, 12288, 1024], P(None, 'blk', 'head')
- next_qkv: float32 [3, 12288, 1024], P(None, 'blk', 'head')
Inputs may be any that keep to these rules, and one draw needn't show every extreme that they name: `block_order`: each half-block index appears once, and stored half-blocks 2i and 2i + 1 hold position blocks that add up to 63. `request_lengths`: the lengths sum to 12288. `enc_lengths`: the lengths sum to 2048.
All inputs are finite; a program needn't handle non-finite values.
Results may differ from a plain program's by a relative error of at most 0.024.
Values may be sent and summed in bfloat16 or wider, within the bound.
A program may use at most 128 MiB of HBM per device.

v0:
```python
import math
import jax
import jax.numpy as jnp
from jax import lax
from jax.sharding import PartitionSpec as P

HEADS = 16
NEGATIVE = -1e30
SCALING = 0.125
EPSILON = 1e-05


def normalize(matrix):
    center = matrix - jnp.mean(matrix, axis=-1, keepdims=True)
    return center * lax.rsqrt(jnp.mean(center * center, axis=-1, keepdims=True) + EPSILON)


def position_of(order_table, indices, halfway):
    slots = jnp.arange(order_table.shape[0], dtype=jnp.int32)
    picked = jnp.sum(
        jnp.where((indices // halfway)[:, None] == slots[None, :], order_table[None, :], 0), axis=1
    )
    return picked * halfway + indices % halfway


def group_of(places, lengths):
    ends = jnp.cumsum(lengths)
    return jnp.sum((places[:, None] >= ends[None, :]).astype(jnp.int32), axis=1)


def online_update(carried, queries, key_rows, value_rows, visible):
    maxima, totals, running = carried
    heads_here = queries.shape[1]
    key_split = key_rows.reshape(key_rows.shape[0], heads_here, -1)
    value_split = value_rows.reshape(value_rows.shape[0], heads_here, -1)
    scores = (
        jnp.einsum("qhd,khd->qhk", queries, key_split, preferred_element_type=jnp.float32) * SCALING
    )
    scores = jnp.where(visible[:, None, :], scores, NEGATIVE)
    updated = jnp.maximum(maxima, jnp.max(scores, axis=2))
    factor = jnp.exp(maxima - updated)
    weights = jnp.exp(scores - updated[:, :, None])
    totals = totals * factor + jnp.sum(weights, axis=2)
    running = running * factor[:, :, None] + jnp.einsum(
        "qhk,khd->qhd",
        weights.astype(jnp.bfloat16),
        value_split,
        preferred_element_type=jnp.float32,
    )
    return (updated, totals, running)


def sweep(
    carried, queries, key_rows, value_rows, key_places, key_groups, query_places, query_groups
):
    length = key_rows.shape[0]
    block_size = math.gcd(length, 2048)
    blocks_count = length // block_size
    key_blocks = key_rows.reshape(blocks_count, block_size, key_rows.shape[1])
    value_blocks = value_rows.reshape(blocks_count, block_size, value_rows.shape[1])
    group_blocks = key_groups.reshape(blocks_count, block_size)
    if key_places is None:
        place_blocks = group_blocks
    else:
        place_blocks = key_places.reshape(blocks_count, block_size)

    def advance(status, element):
        key_block, value_block, place_block, group_block = element
        visible = group_block[None, :] == query_groups[:, None]
        if key_places is None:
            return (online_update(status, queries, key_block, value_block, visible), None)
        visible = visible & (place_block[None, :] <= query_places[:, None])
        updated = online_update(status, queries, key_block, value_block, visible)
        return (updated, None)

    carried, unused = lax.scan(
        advance, carried, (key_blocks, value_blocks, place_blocks, group_blocks)
    )
    return carried


def empty_state(count_q, heads_here, head_width):
    return (
        jnp.full((count_q, heads_here), NEGATIVE, jnp.float32),
        jnp.zeros((count_q, heads_here), jnp.float32),
        jnp.zeros((count_q, heads_here, head_width), jnp.float32),
    )


def finish(carried):
    maxima, totals, running = carried
    return (running / totals[:, :, None]).reshape(running.shape[0], -1).astype(jnp.bfloat16)


def on_device(
    tokens,
    block_order,
    request_lengths,
    enc_lengths,
    w_qkv,
    w_out,
    enc_kv,
    w_cq,
    w_co,
    w_up,
    w_down,
    w_next,
):
    rows_here = tokens.shape[0]
    model_width = tokens.shape[1]
    group_size = lax.axis_size("head")
    cycle_size = lax.axis_size("blk")
    block_rows = rows_here * group_size
    halfway = block_rows // 2
    group_width = w_qkv.shape[2]
    head_width = model_width // HEADS
    group_heads = group_width // head_width
    gathered = lax.all_gather(tokens, "head", axis=0, tiled=True)
    projected = jnp.einsum(
        "td,cde->cte", gathered, w_qkv, preferred_element_type=jnp.float32
    ).astype(jnp.bfloat16)
    cycle_index = lax.axis_index("blk")
    block_start = cycle_index * block_rows
    query_places = position_of(
        block_order, block_start + jnp.arange(block_rows, dtype=jnp.int32), halfway
    )
    query_groups = group_of(query_places, request_lengths)
    queries = projected[0].reshape(block_rows, group_heads, head_width)
    start_state = empty_state(block_rows, group_heads, head_width)
    slots = jnp.arange(2 * cycle_size, dtype=jnp.int32)
    holders = jnp.sum(jnp.where(block_order[:, None] == slots[None, :], slots[:, None], 0), axis=0)
    start_carry = (start_state, jnp.zeros((1,), jnp.bfloat16))
    shards = (
        lax.all_gather(projected[1], "blk", axis=0, tiled=True),
        lax.all_gather(projected[2], "blk", axis=0, tiled=True),
    )
    shard_length = shards[0].shape[0]
    key_places = position_of(block_order, jnp.arange(shard_length, dtype=jnp.int32), halfway)
    key_groups = group_of(key_places, request_lengths)
    final_state = sweep(
        start_carry[0],
        queries,
        shards[0],
        shards[1],
        key_places,
        key_groups,
        query_places,
        query_groups,
    )
    attended = finish(final_state)
    pair = lax.dynamic_slice_in_dim(block_order, 2 * cycle_index, 2, 0)
    targets = pair // 2
    halves = projected[1:].reshape(2, 2, halfway, group_width)
    cycle_slots = jnp.arange(cycle_size, dtype=jnp.int32)
    outgoing = jnp.where(
        (cycle_slots == targets[0])[None, :, None, None],
        halves[:, 0][:, None],
        jnp.where(
            (cycle_slots == targets[1])[None, :, None, None],
            halves[:, 1][:, None],
            jnp.zeros((), jnp.bfloat16),
        ),
    )
    incoming = lax.all_to_all(outgoing, "blk", split_axis=1, concat_axis=1, tiled=True)
    first_source = lax.dynamic_index_in_dim(holders, 2 * cycle_index, 0, keepdims=False) // 2
    second_source = lax.dynamic_index_in_dim(holders, 2 * cycle_index + 1, 0, keepdims=False) // 2
    cache = jnp.concatenate(
        [
            lax.dynamic_index_in_dim(incoming, first_source, 1, keepdims=False),
            lax.dynamic_index_in_dim(incoming, second_source, 1, keepdims=False),
        ],
        axis=1,
    )
    mixed = lax.psum_scatter(
        jnp.dot(attended, w_out, preferred_element_type=jnp.float32),
        "head",
        scatter_dimension=0,
        tiled=True,
    )
    hidden = normalize(mixed + tokens.astype(jnp.float32))
    hidden_b = hidden.astype(jnp.bfloat16)
    member = lax.axis_index("head")
    own_places = lax.dynamic_slice_in_dim(query_places, member * rows_here, rows_here, 0)
    own_groups = group_of(own_places, request_lengths)
    cross_query = jnp.dot(hidden_b, w_cq, preferred_element_type=jnp.float32).astype(jnp.bfloat16)
    cross_split = cross_query.reshape(rows_here, HEADS, head_width)
    widened = lax.all_gather(enc_kv, "head", axis=2, tiled=True)
    shards = lax.all_gather(widened, "blk", axis=1, tiled=True)
    shard_length = shards.shape[1]
    encoder_groups = group_of(jnp.arange(shard_length, dtype=jnp.int32), enc_lengths)
    crossed = finish(
        sweep(
            empty_state(rows_here, HEADS, head_width),
            cross_split,
            shards[0],
            shards[1],
            None,
            encoder_groups,
            None,
            own_groups,
        )
    )
    summed = jnp.dot(crossed, w_co, preferred_element_type=jnp.float32)
    second = normalize(summed + hidden)
    second_b = second.astype(jnp.bfloat16)
    inner = jax.nn.gelu(
        jnp.dot(second_b, w_up, preferred_element_type=jnp.float32), approximate=False
    ).astype(jnp.bfloat16)
    output = normalize(jnp.dot(inner, w_down, preferred_element_type=jnp.float32) + second)
    output_b = output.astype(jnp.bfloat16)
    block_output = lax.all_gather(output_b, "head", axis=0, tiled=True)
    next_qkv = jnp.einsum("td,cde->cte", block_output, w_next, preferred_element_type=jnp.float32)
    return (output, cache, next_qkv)


def solution(mesh):
    in_specs = (
        P(("blk", "head"), None),
        P(),
        P(),
        P(),
        P(None, None, "head"),
        P("head", None),
        P(None, "blk", "head"),
        P(),
        P(),
        P(),
        P(),
        P(None, None, "head"),
    )
    out_specs = (P(("blk", "head"), None), P(None, "blk", "head"), P(None, "blk", "head"))
    return jax.shard_map(
        on_device, mesh=mesh, in_specs=in_specs, out_specs=out_specs, check_vma=False
    )
```

profile of v0, /device:TPU:1, one launch (start us, length us, event | category | flops | bytes accessed | tf_op | source)
XLA Modules:
  0.0 678.4 jit_solution(2549490070128636175)
XLA Ops:
  7.2 10.7 %all_gather.18 = bf16[384,1024]{1,0:T(8,128)(2,1)S(1)} all-gather(bf16[96,1024]{1,0:T(8,128)(2,1)} %param.14), channel_id=1, replica_groups=mesh['blk'=32,'head'=4] {'head'}, dimensions={0}, use_global_device_ids=true | all-gather | bytes 983040 | tf_op jit(solution)/shard_map/all_gather | solution.py:118
  25.4 97.8 %all-gather.8.cloned.1.call-done = bf16[1,12288,256]{1,2,0:T(8,128)(2,1)} async-done(((bf16[1,384,256]{1,2,0:T(8,128)(2,1)}), bf16[1,12288,256]{1,2,0:T(8,128)(2,1)}) %all-gather.8.cloned.1.call-update) | async-done | bytes 6291472 | tf_op jit(solution)/shard_map/all_gather | solution.py:134
  123.3 8.7 %copy.36 = bf16[1,12288,256]{2,1,0:T(8,128)(2,1)} copy(bf16[1,12288,256]{1,2,0:T(8,128)(2,1)} %all-gather.8.cloned.1.call-done) | data formatting | bytes 12582912 | tf_op jit(solution)/shard_map/all_gather | solution.py:134
  132.0 92.0 %all-gather.10.cloned.1.call-done = bf16[1,12288,256]{1,2,0:T(8,128)(2,1)} async-done(((bf16[1,384,256]{1,2,0:T(8,128)(2,1)}), bf16[1,12288,256]{1,2,0:T(8,128)(2,1)}) %all-gather.10.cloned.1.call-update) | async-done | bytes 6291472 | tf_op jit(solution)/shard_map/all_gather | solution.py:135
  224.0 8.6 %copy.37 = bf16[1,12288,256]{2,1,0:T(8,128)(2,1)} copy(bf16[1,12288,256]{1,2,0:T(8,128)(2,1)} %all-gather.10.cloned.1.call-done) | data formatting | bytes 12582912 | tf_op jit(solution)/shard_map/all_gather | solution.py:135
  232.6 196.6 %while.3 = (s32[]{:T(128)}, f32[384,4]{0,1:T(4,128)S(1)}, f32[384,4]{0,1:T(4,128)S(1)}, f32[384,4,64]{0,2,1:T(8,128)S(1)}, s32[6,2048]{1,0:T(8,128)}, /*index=5*...) while((s32[]{:T(128)}, f32[384,4]{0,1:T(4,128)S(1)}, ...), condition=%wide.region_11.12_spmd.clone, body=%wide.region_8.11_spmd.clone.sunk | while | flops 842571264 | bytes 52513932 | solution.py:76
  240.3 8.1 %fusion.171 = (f32[384,4]{0,1:T(4,128)S(1)}, f32[4,2048,384]{2,1,0:T(8,128)}) fusion(pred[384,2048]{0,1:T(8,128)(4,1)S(1)} %compare_and_fusion.2, bf16[2048,4,64]{0,2,1:T(8,128)(2,1)} %bitcast.119, bf16[384,4,64]{0,2,1:T(8,128)(2,1)S(1)} %get-tuple-element.334), kind=kOutput, calls=%fused_computation.4.clone.1 | convolution fusion | flops 412088832 | bytes 14620672 | tf_op jit(solution)/shard_map/while/body/eval_jaxpr/qhd,khd->qhk/dot_general | solution.py:37
  248.4 6.3 fusion.172
  257.1 8.3 %fusion.174 = f32[384,4,64]{0,2,1:T(8,128)S(1)} fusion(bf16[2048,4,64]{0,2,1:T(8,128)(2,1)} %bitcast.120, f32[4,2048,384]{2,1,0:T(8,128)} %get-tuple-element.295, f32[384,4]{0,1:T(4,128)S(1)} %select_maximum_fusion.2, pred[384,2048]{0,1:T(8,128)(4,1)S(1)} %compare_and_fusion.2, f32[384,4,64]{0,2,1:T(8,128)S(1)} %get-tuple-element.315, ...), kind=kOutput, calls=%fused_computation.9.clone.1 | convolution fusion | flops 415531008 | bytes 15216641 | tf_op jit(solution)/shard_map/while/body/eval_jaxpr/qhk,khd->qhd/dot_general | solution.py:44
  273.1 8.1 %fusion.171 = (f32[384,4]{0,1:T(4,128)S(1)}, f32[4,2048,384]{2,1,0:T(8,128)}) fusion(pred[384,2048]{0,1:T(8,128)(4,1)S(1)} %compare_and_fusion.2, bf16[2048,4,64]{0,2,1:T(8,128)(2,1)} %bitcast.119, bf16[384,4,64]{0,2,1:T(8,128)(2,1)S(1)} %get-tuple-element.334), kind=kOutput, calls=%fused_computation.4.clone.1 | convolution fusion | flops 412088832 | bytes 14620672 | tf_op jit(solution)/shard_map/while/body/eval_jaxpr/qhd,khd->qhk/dot_general | solution.py:37
  281.2 6.3 fusion.172
  289.8 8.3 %fusion.174 = f32[384,4,64]{0,2,1:T(8,128)S(1)} fusion(bf16[2048,4,64]{0,2,1:T(8,128)(2,1)} %bitcast.120, f32[4,2048,384]{2,1,0:T(8,128)} %get-tuple-element.295, f32[384,4]{0,1:T(4,128)S(1)} %select_maximum_fusion.2, pred[384,2048]{0,1:T(8,128)(4,1)S(1)} %compare_and_fusion.2, f32[384,4,64]{0,2,1:T(8,128)S(1)} %get-tuple-element.315, ...), kind=kOutput, calls=%fused_computation.9.clone.1 | convolution fusion | flops 415531008 | bytes 15216641 | tf_op jit(solution)/shard_map/while/body/eval_jaxpr/qhk,khd->qhd/dot_general | solution.py:44
  305.9 8.1 %fusion.171 = (f32[384,4]{0,1:T(4,128)S(1)}, f32[4,2048,384]{2,1,0:T(8,128)}) fusion(pred[384,2048]{0,1:T(8,128)(4,1)S(1)} %compare_and_fusion.2, bf16[2048,4,64]{0,2,1:T(8,128)(2,1)} %bitcast.119, bf16[384,4,64]{0,2,1:T(8,128)(2,1)S(1)} %get-tuple-element.334), kind=kOutput, calls=%fused_computation.4.clone.1 | convolution fusion | flops 412088832 | bytes 14620672 | tf_op jit(solution)/shard_map/while/body/eval_jaxpr/qhd,khd->qhk/dot_general | solution.py:37
  313.9 6.3 fusion.172
  322.6 8.3 %fusion.174 = f32[384,4,64]{0,2,1:T(8,128)S(1)} fusion(bf16[2048,4,64]{0,2,1:T(8,128)(2,1)} %bitcast.120, f32[4,2048,384]{2,1,0:T(8,128)} %get-tuple-element.295, f32[384,4]{0,1:T(4,128)S(1)} %select_maximum_fusion.2, pred[384,2048]{0,1:T(8,128)(4,1)S(1)} %compare_and_fusion.2, f32[384,4,64]{0,2,1:T(8,128)S(1)} %get-tuple-element.315, ...), kind=kOutput, calls=%fused_computation.9.clone.1 | convolution fusion | flops 415531008 | bytes 15216641 | tf_op jit(solution)/shard_map/while/body/eval_jaxpr/qhk,khd->qhd/dot_general | solution.py:44
  338.6 8.1 %fusion.171 = (f32[384,4]{0,1:T(4,128)S(1)}, f32[4,2048,384]{2,1,0:T(8,128)}) fusion(pred[384,2048]{0,1:T(8,128)(4,1)S(1)} %compare_and_fusion.2, bf16[2048,4,64]{0,2,1:T(8,128)(2,1)} %bitcast.119, bf16[384,4,64]{0,2,1:T(8,128)(2,1)S(1)} %get-tuple-element.334), kind=kOutput, calls=%fused_computation.4.clone.1 | convolution fusion | flops 412088832 | bytes 14620672 | tf_op jit(solution)/shard_map/while/body/eval_jaxpr/qhd,khd->qhk/dot_general | solution.py:37
  346.7 6.3 fusion.172
  355.4 8.3 %fusion.174 = f32[384,4,64]{0,2,1:T(8,128)S(1)} fusion(bf16[2048,4,64]{0,2,1:T(8,128)(2,1)} %bitcast.120, f32[4,2048,384]{2,1,0:T(8,128)} %get-tuple-element.295, f32[384,4]{0,1:T(4,128)S(1)} %select_maximum_fusion.2, pred[384,2048]{0,1:T(8,128)(4,1)S(1)} %compare_and_fusion.2, f32[384,4,64]{0,2,1:T(8,128)S(1)} %get-tuple-element.315, ...), kind=kOutput, calls=%fused_computation.9.clone.1 | convolution fusion | flops 415531008 | bytes 15216641 | tf_op jit(solution)/shard_map/while/body/eval_jaxpr/qhk,khd->qhd/dot_general | solution.py:44
  371.4 8.1 %fusion.171 = (f32[384,4]{0,1:T(4,128)S(1)}, f32[4,2048,384]{2,1,0:T(8,128)}) fusion(pred[384,2048]{0,1:T(8,128)(4,1)S(1)} %compare_and_fusion.2, bf16[2048,4,64]{0,2,1:T(8,128)(2,1)} %bitcast.119, bf16[384,4,64]{0,2,1:T(8,128)(2,1)S(1)} %get-tuple-element.334), kind=kOutput, calls=%fused_computation.4.clone.1 | convolution fusion | flops 412088832 | bytes 14620672 | tf_op jit(solution)/shard_map/while/body/eval_jaxpr/qhd,khd->qhk/dot_general | solution.py:37
  379.5 6.3 fusion.172
  388.1 8.3 %fusion.174 = f32[384,4,64]{0,2,1:T(8,128)S(1)} fusion(bf16[2048,4,64]{0,2,1:T(8,128)(2,1)} %bitcast.120, f32[4,2048,384]{2,1,0:T(8,128)} %get-tuple-element.295, f32[384,4]{0,1:T(4,128)S(1)} %select_maximum_fusion.2, pred[384,2048]{0,1:T(8,128)(4,1)S(1)} %compare_and_fusion.2, f32[384,4,64]{0,2,1:T(8,128)S(1)} %get-tuple-element.315, ...), kind=kOutput, calls=%fused_computation.9.clone.1 | convolution fusion | flops 415531008 | bytes 15216641 | tf_op jit(solution)/shard_map/while/body/eval_jaxpr/qhk,khd->qhd/dot_general | solution.py:44
  404.2 8.1 %fusion.171 = (f32[384,4]{0,1:T(4,128)S(1)}, f32[4,2048,384]{2,1,0:T(8,128)}) fusion(pred[384,2048]{0,1:T(8,128)(4,1)S(1)} %compare_and_fusion.2, bf16[2048,4,64]{0,2,1:T(8,128)(2,1)} %bitcast.119, bf16[384,4,64]{0,2,1:T(8,128)(2,1)S(1)} %get-tuple-element.334), kind=kOutput, calls=%fused_computation.4.clone.1 | convolution fusion | flops 412088832 | bytes 14620672 | tf_op jit(solution)/shard_map/while/body/eval_jaxpr/qhd,khd->qhk/dot_general | solution.py:37
  412.2 6.3 fusion.172
  420.9 8.3 %fusion.174 = f32[384,4,64]{0,2,1:T(8,128)S(1)} fusion(bf16[2048,4,64]{0,2,1:T(8,128)(2,1)} %bitcast.120, f32[4,2048,384]{2,1,0:T(8,128)} %get-tuple-element.295, f32[384,4]{0,1:T(4,128)S(1)} %select_maximum_fusion.2, pred[384,2048]{0,1:T(8,128)(4,1)S(1)} %compare_and_fusion.2, f32[384,4,64]{0,2,1:T(8,128)S(1)} %get-tuple-element.315, ...), kind=kOutput, calls=%fused_computation.9.clone.1 | convolution fusion | flops 415531008 | bytes 15216641 | tf_op jit(solution)/shard_map/while/body/eval_jaxpr/qhk,khd->qhd/dot_general | solution.py:44
  432.0 7.6 %all_gather.21 = bf16[2,64,1024]{2,1,0:T(8,128)(2,1)} all-gather(bf16[2,64,256]{2,1,0:T(8,128)(2,1)S(1)} %copy-done.5), channel_id=1, replica_groups=mesh['blk'=32,'head'=4] {'head'}, dimensions={2}, use_global_device_ids=true | all-gather | bytes 327680 | tf_op jit(solution)/shard_map/all_gather | solution.py:187
  457.0 85.6 %all-to-all-done = bf16[2,32,192,256]{3,2,0,1:T(8,128)(2,1)} async-done(((bf16[2,32,192,256]{3,2,0,1:T(8,128)(2,1)}), bf16[2,32,192,256]{3,2,0,1:T(8,128)(2,1)}, u32[]{:S(2)}, u32[]{:S(2)}) %all-to-all-start) | async-done | bytes 6291488 | tf_op jit(solution)/shard_map/all_to_all | solution.py:164
  549.3 62.4 %all-gather.6.cloned.1.call-done = bf16[2,2048,1024]{2,1,0:T(8,128)(2,1)} async-done(((bf16[2,64,1024]{2,1,0:T(8,128)(2,1)}), bf16[2,2048,1024]{2,1,0:T(8,128)(2,1)}) %all-gather.6.cloned.1.call-update) | async-done | bytes 8388624 | tf_op jit(solution)/shard_map/all_gather | solution.py:188
  617.6 6.5 copy.41
  633.2 6.5 copy.42
  639.7 9.5 %fusion.41 = bf16[96,16,64]{0,2,1:T(8,128)(2,1)S(1)} fusion(bf16[2048,16,64]{0,2,1:T(8,128)(2,1)} %bitcast.125, f32[16,96,2048]{2,1,0:T(8,128)} %copy-done.1, f32[96,16]{0,1:T(8,128)S(1)} %broadcast_maximum_fusion, pred[96,2048]{1,0:T(8,128)(4,1)S(1)} %broadcast_compare_fusion, f32[96,16]{0,1:T(8,128)S(1)} %get-tuple-element.203, ...), kind=kOutput, calls=%fused_computation.60 | convolution fusion | flops 415531008 | bytes 17188864 | tf_op jit(solution)/shard_map/while/body/eval_jaxpr/qhk,khd->qhd/dot_general | solution.py:44
  650.1 10.2 %fusion.142 = (f32[96]{0:T(128)S(1)}, f32[96,1024]{1,0:T(8,128)S(1)}) fusion(f32[96]{0:T(128)S(1)} %add_rsqrt_fusion.1, f32[96,1024]{1,0:T(8,128)S(1)} %get-tuple-element.211, f32[96]{0:T(128)S(1)} %broadcast_multiply_fusion.2, bf16[4096,1024]{1,0:T(8,128)(2,1)} %param.24, bf16[1024,4096]{1,0:T(8,128)(2,1)} %param.23), kind=kOutput, calls=%fused_computation.204 | convolution fusion | flops 1636859776 | bytes 17564800 | tf_op jit(solution)/shard_map/dot_general | solution.py:209
  661.4 8.7 %all_gather.23 = bf16[384,1024]{1,0:T(8,128)(2,1)S(1)} all-gather(bf16[96,1024]{1,0:T(8,128)(2,1)S(1)} %get-tuple-element.183), channel_id=1, replica_groups=mesh['blk'=32,'head'=4] {'head'}, dimensions={0}, use_global_device_ids=true | all-gather | bytes 983040 | tf_op jit(solution)/shard_map/all_gather | solution.py:211
  (134 shorter events, 108.1 us)
Async XLA Ops:
  7.2 642.1 %copy-start = (bf16[1024,1024]{1,0:T(8,128)(2,1)S(1)}, bf16[1024,1024]{1,0:T(8,128)(2,1)}, u32[]{:S(2)}) copy-start(bf16[1024,1024]{1,0:T(8,128)(2,1)} %param.22) | copy-start | bytes 6291460
  7.2 116.1 %all-gather.8.cloned.1.call-start = ((), (), s32[]{:S(2)}) async-start(), calls=%async_computation.4 | async-start | bytes 6488064 | tf_op jit(solution)/shard_map/all_gather | solution.py:134
  17.9 4.9 copy-start.8
  17.9 5.1 copy-start.6
  20.4 0.8 copy-start.4
  22.0 201.9 %all-gather.10.cloned.1.call-start = ((), (), s32[]{:S(2)}) async-start(), calls=%async_computation.5 | async-start | bytes 6488064 | tf_op jit(solution)/shard_map/all_gather | solution.py:135
  22.8 521.7 %reduce-scatter.2.cloned.1.call-start = ((), (), s32[]{:S(2)}) async-start(), calls=%async_computation.2 | async-start | bytes 1966080 | tf_op jit(solution)/shard_map/reduce_scatter | solution.py:174
  429.2 2.8 copy-start.5
  429.3 10.4 %slice-start = ((bf16[3,384,256]{1,2,0:T(8,128)(2,1)}), bf16[2,384,256]{1,2,0:T(8,128)(2,1)S(1)}, s32[]{:S(2)}) async-start(bf16[3,384,256]{1,2,0:T(8,128)(2,1)} %copy-done.4), calls=%async_computation.6 | async-start | bytes 786432 | tf_op jit(solution)/shard_map/slice | solution.py:153
  432.0 179.7 %all-gather.6.cloned.1.call-start = ((), (), s32[]{:S(2)}) async-start(), calls=%async_computation.3 | async-start | bytes 8650752 | tf_op jit(solution)/shard_map/all_gather | solution.py:188
  445.2 11.3 %copy-start.9 = (s32[9]{0:T(128)S(1)}, s32[9]{0:T(128)}, u32[]{:S(2)}) copy-start(s32[9]{0:T(128)} %param.17) | copy-start | bytes 112
  445.2 99.3 %copy-start.3 = (bf16[96,1024]{1,0:T(8,128)(2,1)S(1)}, bf16[96,1024]{1,0:T(8,128)(2,1)}, u32[]{:S(2)}) copy-start(bf16[96,1024]{1,0:T(8,128)(2,1)} %param.14) | copy-start | bytes 589828
  445.2 97.5 %all-to-all-start = ((bf16[2,32,192,256]{3,2,0,1:T(8,128)(2,1)}), bf16[2,32,192,256]{3,2,0,1:T(8,128)(2,1)}, u32[]{:S(2)}, u32[]{:S(2)}) async-start(bf16[2,32,192,256]{3,2,0,1:T(8,128)(2,1)} %select_select_fusion), calls=%async_computation.1 | async-start | bytes 12582912 | tf_op jit(solution)/shard_map/all_to_all | solution.py:164
  628.7 4.6 copy-start.1
  639.7 9.5 %copy-start.2 = (f32[96,1024]{1,0:T(8,128)S(1)}, f32[96,1024]{1,0:T(8,128)}, u32[]{:S(2)}) copy-start(f32[96,1024]{1,0:T(8,128)} %reduce-scatter.2.cloned.1.call-done) | copy-start | bytes 1179652
  660.3 9.8 %copy-start.7 = (bf16[3,1024,256]{2,1,0:T(8,128)(2,1)S(1)}, bf16[3,1024,256]{2,1,0:T(8,128)(2,1)}, u32[]{:S(2)}) copy-start(bf16[3,1024,256]{2,1,0:T(8,128)(2,1)} %param.25) | copy-start | bytes 4718596
Sparse Core Ops, SparseCore 0:
  22.2 101.0 all-gather.7
  126.6 97.2 all-gather.9
  432.1 22.4 reduce-scatter.1
  457.6 154.0 all-gather.5
where the time goes:
time: 681 us; the launch traced here: 678 us
  waiting for transfers between devices  339 us (50%)
  matrix products  132 us (19%)
  local copies, waits for them, and re-layouts  94.2 us (14%)
  other arithmetic  61.5 us (9%)
  blocking collectives  27.1 us (4%)
  between operations  19.3 us (3%)
    all_gather x1, waiting for transfers between devices, on_device(): lax.all_gather(projected[1], 'blk', axis=0, tiled=True)  97.8 us
    all_gather x1, waiting for transfers between devices, on_device(): lax.all_gather(projected[2], 'blk', axis=0, tiled=True)  92 us
    all_to_all x1, waiting for transfers between devices, on_device(): lax.all_to_all(outgoing, 'blk', split_axis=1, concat_axis=1, tiled=True)  85.6 us
    all_gather x1, waiting for transfers between devices, on_device(): shards = lax.all_gather(widened, 'blk', axis=1, tiled=True)  62.4 us
    dot_general x7, matrix products, online_update(): jnp.einsum('qhk,khd->qhd', weights.astype(jnp.bfloat16), value_split, pre...  59.2 us
    dot_general x7, matrix products, online_update(): jnp.einsum('qhd,khd->qhk', queries, key_split, preferred_element_type=jnp...  52.9 us
    dynamic_slice x24, local copies, waits for them, and re-layouts, sweep(): lax.scan(advance, carried, (key_blocks, value_blocks, place_blocks, group...  51.5 us
    reduce_sum x7, other arithmetic, online_update(): totals = totals * factor + jnp.sum(weights, axis=2)  40.9 us
  transfers between devices with their start and end apart: 5, of which 4 were waited for; matrix products, arithmetic and copies ran while one was open for 4% of the time, Pallas kernels for 0%

commit v1 on v0

--- a/solution.py
+++ b/solution.py
@@ -131,7 +131,9 @@
     holders = jnp.sum(jnp.where(block_order[:, None] == slots[None, :], slots[:, None], 0), axis=0)
     start_carry = (start_state, jnp.zeros((1,), jnp.bfloat16))
     shards = (
-        lax.all_gather(projected[1], "blk", axis=0, tiled=True),
+        jnp.concatenate(
+            lax.all_to_all(jnp.stack([projected[1]] * lax.axis_size("blk")), "blk", 0, 0), axis=0
+        ),
         lax.all_gather(projected[2], "blk", axis=0, tiled=True),
     )
     shard_length = shards[0].shape[0]

time: 681 us -> 643 us (0.944)
  waiting for transfers between devices: 339 us -> 296 us
  starting transfers between devices: 5.43 us -> 15.9 us
    all_gather x1 -> x0, waiting for transfers between devices: 97.8 us -> none  [on_device(): lax.all_gather(projected[1], 'blk', axis=0, tiled=True)]
    all_gather x1, waiting for transfers between devices: 92 us -> 147 us  [on_device(): lax.all_gather(projected[2], 'blk', axis=0, tiled=True)]
    all_to_all x0 -> x1, starting transfers between devices: none -> 10.3 us  [on_device(): lax.all_to_all(jnp.stack([projected[1]] * lax.axis_size('blk')), 'blk', 0...]
    all_gather x1 -> x0, local copies, waits for them, and re-layouts: 8.68 us -> none  [on_device(): lax.all_gather(projected[1], 'blk', axis=0, tiled=True)]
  transfers between devices with their start and end apart: 5 -> 5, of which waited for: 4 -> 3; matrix products, arithmetic and copies ran while one was open for 4% -> 4% of each run, Pallas kernels for 0% -> 0%
where the time goes in v1:
time: 643 us; the launch traced here: 641 us
  waiting for transfers between devices  296 us (46%)
  matrix products  132 us (21%)
  local copies, waits for them, and re-layouts  89 us (14%)
  other arithmetic  61.5 us (10%)
  blocking collectives  27.1 us (4%)
  between operations  19.3 us (3%)
  starting transfers between devices  15.9 us (2%)
    all_gather x1, waiting for transfers between devices, on_device(): lax.all_gather(projected[2], 'blk', axis=0, tiled=True)  147 us
    all_to_all x1, waiting for transfers between devices, on_device(): lax.all_to_all(outgoing, 'blk', split_axis=1, concat_axis=1, tiled=True)  85.5 us
    all_gather x1, waiting for transfers between devices, on_device(): shards = lax.all_gather(widened, 'blk', axis=1, tiled=True)  62.8 us
    dot_general x7, matrix products, online_update(): jnp.einsum('qhk,khd->qhd', weights.astype(jnp.bfloat16), value_split, pre...  59.2 us
    dot_general x7, matrix products, online_update(): jnp.einsum('qhd,khd->qhk', queries, key_split, preferred_element_type=jnp...  52.9 us
    dynamic_slice x24, local copies, waits for them, and re-layouts, sweep(): lax.scan(advance, carried, (key_blocks, value_blocks, place_blocks, group...  51.5 us
    reduce_sum x7, other arithmetic, online_update(): totals = totals * factor + jnp.sum(weights, axis=2)  40.9 us
  transfers between devices with their start and end apart: 5, of which 3 were waited for; matrix products, arithmetic and copies ran while one was open for 4% of the time, Pallas kernels for 0%

profile of v1, /device:TPU:1, one launch (start us, length us, event | category | flops | bytes accessed | tf_op | source)
XLA Modules:
  0.0 640.7 jit_solution(8386161504564473757)
XLA Ops:
  7.2 10.7 %all_gather.15 = bf16[384,1024]{1,0:T(8,128)(2,1)S(1)} all-gather(bf16[96,1024]{1,0:T(8,128)(2,1)} %param.14), channel_id=1, replica_groups=mesh['blk'=32,'head'=4] {'head'}, dimensions={0}, use_global_device_ids=true | all-gather | bytes 983040 | tf_op jit(solution)/shard_map/all_gather | solution.py:118
  25.5 10.3 %all-to-all-start = ((bf16[32,384,256]{2,1,0:T(8,128)(2,1)}), bf16[32,384,256]{2,1,0:T(8,128)(2,1)}, u32[]{:S(2)}, u32[]{:S(2)}) async-start(bf16[32,384,256]{2,1,0:T(8,128)(2,1)} %stack.3), calls=%async_computation | async-start | bytes 12582912 | tf_op jit(solution)/shard_map/all_to_all | solution.py:135
  38.6 147.4 %all-gather.6.cloned.1.call-done = bf16[1,12288,256]{1,2,0:T(8,128)(2,1)} async-done(((bf16[1,384,256]{1,2,0:T(8,128)(2,1)}), bf16[1,12288,256]{1,2,0:T(8,128)(2,1)}) %all-gather.6.cloned.1.call-update) | async-done | bytes 6291472 | tf_op jit(solution)/shard_map/all_gather | solution.py:137
  186.0 8.6 %copy.37 = bf16[1,12288,256]{2,1,0:T(8,128)(2,1)} copy(bf16[1,12288,256]{1,2,0:T(8,128)(2,1)} %all-gather.6.cloned.1.call-done) | data formatting | bytes 12582912 | tf_op jit(solution)/shard_map/all_gather | solution.py:137
  194.6 196.6 %while.3 = (s32[]{:T(128)}, f32[384,4]{0,1:T(4,128)S(1)}, f32[384,4]{0,1:T(4,128)S(1)}, f32[384,4,64]{0,2,1:T(8,128)S(1)}, s32[6,2048]{1,0:T(8,128)}, /*index=5*...) while((s32[]{:T(128)}, f32[384,4]{0,1:T(4,128)S(1)}, ...), condition=%wide.region_11.12_spmd.clone, body=%wide.region_8.11_spmd.clone.sunk | while | flops 842571264 | bytes 52513932 | solution.py:76
  202.4 8.1 %fusion.171 = (f32[384,4]{0,1:T(4,128)S(1)}, f32[4,2048,384]{2,1,0:T(8,128)}) fusion(pred[384,2048]{0,1:T(8,128)(4,1)S(1)} %compare_and_fusion.2, bf16[2048,4,64]{0,2,1:T(8,128)(2,1)} %bitcast.121, bf16[384,4,64]{0,2,1:T(8,128)(2,1)S(1)} %get-tuple-element.334), kind=kOutput, calls=%fused_computation.4.clone.1 | convolution fusion | flops 412088832 | bytes 14620672 | tf_op jit(solution)/shard_map/while/body/eval_jaxpr/qhd,khd->qhk/dot_general | solution.py:37
  210.4 6.3 fusion.172
  219.1 8.3 %fusion.174 = f32[384,4,64]{0,2,1:T(8,128)S(1)} fusion(bf16[2048,4,64]{0,2,1:T(8,128)(2,1)} %bitcast.122, f32[4,2048,384]{2,1,0:T(8,128)} %get-tuple-element.295, f32[384,4]{0,1:T(4,128)S(1)} %select_maximum_fusion.2, pred[384,2048]{0,1:T(8,128)(4,1)S(1)} %compare_and_fusion.2, f32[384,4,64]{0,2,1:T(8,128)S(1)} %get-tuple-element.315, ...), kind=kOutput, calls=%fused_computation.9.clone.1 | convolution fusion | flops 415531008 | bytes 15216641 | tf_op jit(solution)/shard_map/while/body/eval_jaxpr/qhk,khd->qhd/dot_general | solution.py:44
  235.1 8.1 %fusion.171 = (f32[384,4]{0,1:T(4,128)S(1)}, f32[4,2048,384]{2,1,0:T(8,128)}) fusion(pred[384,2048]{0,1:T(8,128)(4,1)S(1)} %compare_and_fusion.2, bf16[2048,4,64]{0,2,1:T(8,128)(2,1)} %bitcast.121, bf16[384,4,64]{0,2,1:T(8,128)(2,1)S(1)} %get-tuple-element.334), kind=kOutput, calls=%fused_computation.4.clone.1 | convolution fusion | flops 412088832 | bytes 14620672 | tf_op jit(solution)/shard_map/while/body/eval_jaxpr/qhd,khd->qhk/dot_general | solution.py:37
  243.2 6.3 fusion.172
  251.9 8.3 %fusion.174 = f32[384,4,64]{0,2,1:T(8,128)S(1)} fusion(bf16[2048,4,64]{0,2,1:T(8,128)(2,1)} %bitcast.122, f32[4,2048,384]{2,1,0:T(8,128)} %get-tuple-element.295, f32[384,4]{0,1:T(4,128)S(1)} %select_maximum_fusion.2, pred[384,2048]{0,1:T(8,128)(4,1)S(1)} %compare_and_fusion.2, f32[384,4,64]{0,2,1:T(8,128)S(1)} %get-tuple-element.315, ...), kind=kOutput, calls=%fused_computation.9.clone.1 | convolution fusion | flops 415531008 | bytes 15216641 | tf_op jit(solution)/shard_map/while/body/eval_jaxpr/qhk,khd->qhd/dot_general | solution.py:44
  267.9 8.1 %fusion.171 = (f32[384,4]{0,1:T(4,128)S(1)}, f32[4,2048,384]{2,1,0:T(8,128)}) fusion(pred[384,2048]{0,1:T(8,128)(4,1)S(1)} %compare_and_fusion.2, bf16[2048,4,64]{0,2,1:T(8,128)(2,1)} %bitcast.121, bf16[384,4,64]{0,2,1:T(8,128)(2,1)S(1)} %get-tuple-element.334), kind=kOutput, calls=%fused_computation.4.clone.1 | convolution fusion | flops 412088832 | bytes 14620672 | tf_op jit(solution)/shard_map/while/body/eval_jaxpr/qhd,khd->qhk/dot_general | solution.py:37
  276.0 6.3 fusion.172
  284.6 8.3 %fusion.174 = f32[384,4,64]{0,2,1:T(8,128)S(1)} fusion(bf16[2048,4,64]{0,2,1:T(8,128)(2,1)} %bitcast.122, f32[4,2048,384]{2,1,0:T(8,128)} %get-tuple-element.295, f32[384,4]{0,1:T(4,128)S(1)} %select_maximum_fusion.2, pred[384,2048]{0,1:T(8,128)(4,1)S(1)} %compare_and_fusion.2, f32[384,4,64]{0,2,1:T(8,128)S(1)} %get-tuple-element.315, ...), kind=kOutput, calls=%fused_computation.9.clone.1 | convolution fusion | flops 415531008 | bytes 15216641 | tf_op jit(solution)/shard_map/while/body/eval_jaxpr/qhk,khd->qhd/dot_general | solution.py:44
  300.7 8.1 %fusion.171 = (f32[384,4]{0,1:T(4,128)S(1)}, f32[4,2048,384]{2,1,0:T(8,128)}) fusion(pred[384,2048]{0,1:T(8,128)(4,1)S(1)} %compare_and_fusion.2, bf16[2048,4,64]{0,2,1:T(8,128)(2,1)} %bitcast.121, bf16[384,4,64]{0,2,1:T(8,128)(2,1)S(1)} %get-tuple-element.334), kind=kOutput, calls=%fused_computation.4.clone.1 | convolution fusion | flops 412088832 | bytes 14620672 | tf_op jit(solution)/shard_map/while/body/eval_jaxpr/qhd,khd->qhk/dot_general | solution.py:37
  308.7 6.3 fusion.172
  317.4 8.3 %fusion.174 = f32[384,4,64]{0,2,1:T(8,128)S(1)} fusion(bf16[2048,4,64]{0,2,1:T(8,128)(2,1)} %bitcast.122, f32[4,2048,384]{2,1,0:T(8,128)} %get-tuple-element.295, f32[384,4]{0,1:T(4,128)S(1)} %select_maximum_fusion.2, pred[384,2048]{0,1:T(8,128)(4,1)S(1)} %compare_and_fusion.2, f32[384,4,64]{0,2,1:T(8,128)S(1)} %get-tuple-element.315, ...), kind=kOutput, calls=%fused_computation.9.clone.1 | convolution fusion | flops 415531008 | bytes 15216641 | tf_op jit(solution)/shard_map/while/body/eval_jaxpr/qhk,khd->qhd/dot_general | solution.py:44
  333.4 8.1 %fusion.171 = (f32[384,4]{0,1:T(4,128)S(1)}, f32[4,2048,384]{2,1,0:T(8,128)}) fusion(pred[384,2048]{0,1:T(8,128)(4,1)S(1)} %compare_and_fusion.2, bf16[2048,4,64]{0,2,1:T(8,128)(2,1)} %bitcast.121, bf16[384,4,64]{0,2,1:T(8,128)(2,1)S(1)} %get-tuple-element.334), kind=kOutput, calls=%fused_computation.4.clone.1 | convolution fusion | flops 412088832 | bytes 14620672 | tf_op jit(solution)/shard_map/while/body/eval_jaxpr/qhd,khd->qhk/dot_general | solution.py:37
  341.5 6.3 fusion.172
  350.2 8.3 %fusion.174 = f32[384,4,64]{0,2,1:T(8,128)S(1)} fusion(bf16[2048,4,64]{0,2,1:T(8,128)(2,1)} %bitcast.122, f32[4,2048,384]{2,1,0:T(8,128)} %get-tuple-element.295, f32[384,4]{0,1:T(4,128)S(1)} %select_maximum_fusion.2, pred[384,2048]{0,1:T(8,128)(4,1)S(1)} %compare_and_fusion.2, f32[384,4,64]{0,2,1:T(8,128)S(1)} %get-tuple-element.315, ...), kind=kOutput, calls=%fused_computation.9.clone.1 | convolution fusion | flops 415531008 | bytes 15216641 | tf_op jit(solution)/shard_map/while/body/eval_jaxpr/qhk,khd->qhd/dot_general | solution.py:44
  366.2 8.1 %fusion.171 = (f32[384,4]{0,1:T(4,128)S(1)}, f32[4,2048,384]{2,1,0:T(8,128)}) fusion(pred[384,2048]{0,1:T(8,128)(4,1)S(1)} %compare_and_fusion.2, bf16[2048,4,64]{0,2,1:T(8,128)(2,1)} %bitcast.121, bf16[384,4,64]{0,2,1:T(8,128)(2,1)S(1)} %get-tuple-element.334), kind=kOutput, calls=%fused_computation.4.clone.1 | convolution fusion | flops 412088832 | bytes 14620672 | tf_op jit(solution)/shard_map/while/body/eval_jaxpr/qhd,khd->qhk/dot_general | solution.py:37
  374.2 6.3 fusion.172
  382.9 8.3 %fusion.174 = f32[384,4,64]{0,2,1:T(8,128)S(1)} fusion(bf16[2048,4,64]{0,2,1:T(8,128)(2,1)} %bitcast.122, f32[4,2048,384]{2,1,0:T(8,128)} %get-tuple-element.295, f32[384,4]{0,1:T(4,128)S(1)} %select_maximum_fusion.2, pred[384,2048]{0,1:T(8,128)(4,1)S(1)} %compare_and_fusion.2, f32[384,4,64]{0,2,1:T(8,128)S(1)} %get-tuple-element.315, ...), kind=kOutput, calls=%fused_computation.9.clone.1 | convolution fusion | flops 415531008 | bytes 15216641 | tf_op jit(solution)/shard_map/while/body/eval_jaxpr/qhk,khd->qhd/dot_general | solution.py:44
  394.0 7.6 %all_gather.17 = bf16[2,64,1024]{2,1,0:T(8,128)(2,1)} all-gather(bf16[2,64,256]{2,1,0:T(8,128)(2,1)S(1)} %copy-done.5), channel_id=1, replica_groups=mesh['blk'=32,'head'=4] {'head'}, dimensions={2}, use_global_device_ids=true | all-gather | bytes 327680 | tf_op jit(solution)/shard_map/all_gather | solution.py:189
  419.0 85.5 %all-to-all-done.1 = bf16[2,32,192,256]{3,2,0,1:T(8,128)(2,1)} async-done(((bf16[2,32,192,256]{3,2,0,1:T(8,128)(2,1)}), bf16[2,32,192,256]{3,2,0,1:T(8,128)(2,1)}, u32[]{:S(2)}, u32[]{:S(2)}) %all-to-all-start.1) | async-done | bytes 6291488 | tf_op jit(solution)/shard_map/all_to_all | solution.py:166
  511.1 62.8 %all-gather.4.cloned.1.call-done = bf16[2,2048,1024]{2,1,0:T(8,128)(2,1)} async-done(((bf16[2,64,1024]{2,1,0:T(8,128)(2,1)}), bf16[2,2048,1024]{2,1,0:T(8,128)(2,1)}) %all-gather.4.cloned.1.call-update) | async-done | bytes 8388624 | tf_op jit(solution)/shard_map/all_gather | solution.py:190
  573.9 5.9 fusion.137
  579.8 6.5 %copy.41 = bf16[1,2048,1024]{1,2,0:T(8,128)(2,1)} copy(bf16[1,2048,1024]{2,1,0:T(8,128)(2,1)} %get-tuple-element.191) | data formatting | bytes 8388608 | tf_op jit(solution)/shard_map/slice | solution.py:197
  595.5 6.5 %copy.42 = bf16[1,2048,1024]{1,2,0:T(8,128)(2,1)} copy(bf16[1,2048,1024]{2,1,0:T(8,128)(2,1)} %get-tuple-element.192) | data formatting | bytes 8388608 | tf_op jit(solution)/shard_map/slice | solution.py:198
  602.0 9.5 %fusion.41 = bf16[96,16,64]{0,2,1:T(8,128)(2,1)S(1)} fusion(bf16[2048,16,64]{0,2,1:T(8,128)(2,1)} %bitcast.126, f32[16,96,2048]{2,1,0:T(8,128)} %copy-done.1, f32[96,16]{0,1:T(8,128)S(1)} %broadcast_maximum_fusion, pred[96,2048]{1,0:T(8,128)(4,1)S(1)} %broadcast_compare_fusion, f32[96,16]{0,1:T(8,128)S(1)} %get-tuple-element.203, ...), kind=kOutput, calls=%fused_computation.60 | convolution fusion | flops 415531008 | bytes 17188864 | tf_op jit(solution)/shard_map/while/body/eval_jaxpr/qhk,khd->qhd/dot_general | solution.py:44
  612.3 10.3 %fusion.142 = (f32[96]{0:T(128)S(1)}, f32[96,1024]{1,0:T(8,128)S(1)}) fusion(f32[96]{0:T(128)S(1)} %add_rsqrt_fusion.1, f32[96,1024]{1,0:T(8,128)S(1)} %get-tuple-element.211, f32[96]{0:T(128)S(1)} %broadcast_multiply_fusion.2, bf16[4096,1024]{1,0:T(8,128)(2,1)} %param.24, bf16[1024,4096]{1,0:T(8,128)(2,1)} %param.23), kind=kOutput, calls=%fused_computation.205 | convolution fusion | flops 1636859776 | bytes 17564800 | tf_op jit(solution)/shard_map/dot_general | solution.py:211
  623.7 8.7 %all_gather.19 = bf16[384,1024]{1,0:T(8,128)(2,1)S(1)} all-gather(bf16[96,1024]{1,0:T(8,128)(2,1)S(1)} %get-tuple-element.183), channel_id=1, replica_groups=mesh['blk'=32,'head'=4] {'head'}, dimensions={0}, use_global_device_ids=true | all-gather | bytes 983040 | tf_op jit(solution)/shard_map/all_gather | solution.py:213
  (134 shorter events, 105.1 us)
Async XLA Ops:
  7.2 604.3 %copy-start = (bf16[1024,1024]{1,0:T(8,128)(2,1)S(1)}, bf16[1024,1024]{1,0:T(8,128)(2,1)}, u32[]{:S(2)}) copy-start(bf16[1024,1024]{1,0:T(8,128)(2,1)} %param.22) | copy-start | bytes 6291460
  7.2 178.8 %all-gather.6.cloned.1.call-start = ((), (), s32[]{:S(2)}) async-start(), calls=%async_computation.5 | async-start | bytes 6488064 | tf_op jit(solution)/shard_map/all_gather | solution.py:137
  20.4 0.8 copy-start.4
  25.5 10.6 %copy-start.8 = (s32[9]{0:T(128)S(1)}, s32[9]{0:T(128)}, u32[]{:S(2)}) copy-start(s32[9]{0:T(128)} %param.16) | copy-start | bytes 112
  25.5 10.8 %copy-start.6 = (s32[64]{0:T(128)S(1)}, s32[64]{0:T(128)}, u32[]{:S(2)}) copy-start(s32[64]{0:T(128)} %param.15) | copy-start | bytes 772
  25.5 169.2 %all-to-all-start = ((bf16[32,384,256]{2,1,0:T(8,128)(2,1)}), bf16[32,384,256]{2,1,0:T(8,128)(2,1)}, u32[]{:S(2)}, u32[]{:S(2)}) async-start(bf16[32,384,256]{2,1,0:T(8,128)(2,1)} %stack.3), calls=%async_computation | async-start | bytes 12582912 | tf_op jit(solution)/shard_map/all_to_all | solution.py:135
  35.8 470.6 %reduce-scatter.2.cloned.1.call-start = ((), (), s32[]{:S(2)}) async-start(), calls=%async_computation.3 | async-start | bytes 1966080 | tf_op jit(solution)/shard_map/reduce_scatter | solution.py:176
  391.2 2.8 copy-start.5
  391.3 10.4 %slice-start = ((bf16[3,384,256]{1,2,0:T(8,128)(2,1)}), bf16[2,384,256]{1,2,0:T(8,128)(2,1)S(1)}, s32[]{:S(2)}) async-start(bf16[3,384,256]{1,2,0:T(8,128)(2,1)} %copy-done.4), calls=%async_computation.6 | async-start | bytes 786432 | tf_op jit(solution)/shard_map/slice | solution.py:155
  394.0 179.9 %all-gather.4.cloned.1.call-start = ((), (), s32[]{:S(2)}) async-start(), calls=%async_computation.4 | async-start | bytes 8650752 | tf_op jit(solution)/shard_map/all_gather | solution.py:190
  407.2 11.3 %copy-start.9 = (s32[9]{0:T(128)S(1)}, s32[9]{0:T(128)}, u32[]{:S(2)}) copy-start(s32[9]{0:T(128)} %param.17) | copy-start | bytes 112
  407.2 99.2 %copy-start.3 = (bf16[96,1024]{1,0:T(8,128)(2,1)S(1)}, bf16[96,1024]{1,0:T(8,128)(2,1)}, u32[]{:S(2)}) copy-start(bf16[96,1024]{1,0:T(8,128)(2,1)} %param.14) | copy-start | bytes 589828
  407.2 97.3 %all-to-all-start.1 = ((bf16[2,32,192,256]{3,2,0,1:T(8,128)(2,1)}), bf16[2,32,192,256]{3,2,0,1:T(8,128)(2,1)}, u32[]{:S(2)}, u32[]{:S(2)}) async-start(bf16[2,32,192,256]{3,2,0,1:T(8,128)(2,1)} %select_select_fusion), calls=%async_computation.2 | async-start | bytes 12582912 | tf_op jit(solution)/shard_map/all_to_all | solution.py:166
  590.9 4.6 copy-start.1
  602.0 9.5 %copy-start.2 = (f32[96,1024]{1,0:T(8,128)S(1)}, f32[96,1024]{1,0:T(8,128)}, u32[]{:S(2)}) copy-start(f32[96,1024]{1,0:T(8,128)} %reduce-scatter.2.cloned.1.call-done) | copy-start | bytes 1179652
  622.6 9.8 %copy-start.7 = (bf16[3,1024,256]{2,1,0:T(8,128)(2,1)S(1)}, bf16[3,1024,256]{2,1,0:T(8,128)(2,1)}, u32[]{:S(2)}) copy-start(bf16[3,1024,256]{2,1,0:T(8,128)(2,1)} %param.25) | copy-start | bytes 4718596
Sparse Core Ops, SparseCore 0:
  22.1 163.8 all-gather.5
  394.1 22.3 reduce-scatter.1
  419.7 154.2 all-gather.3
